TPU v7x, 32 devices: a whole 2x2x4 slice. The times are simulated.
32 devices in a mesh: dp: 16 (over z, y, x), fsdp: 2 (over core).
Axes of the slice: x: 2, y: 2, z: 4, core: 2. Of those that a mesh axis runs over, the one named last changes fastest.
Arguments:
- hidden_in: bfloat16 [32, 1024, 768], P(('dp', 'fsdp')), may hold values from -6 to 6
- row_grad: bfloat16 [32, 1024, 768], P(('dp', 'fsdp')), may hold values from -6 to 6
- segment_ids: int32 [32, 1024], P(('dp', 'fsdp')), may hold values from 0 to 15, as said below
- query_cls: int32 [32, 8], P(('dp', 'fsdp')), may hold values from 0 to 1022, as said below
- passage_cls: int32 [32, 8], P(('dp', 'fsdp')), may hold values from 16 to 1023, as said below
- positives: int32 [256], replicated, may hold values from 0 to 255
- w_query: float32 [768, 768], P(('dp', 'fsdp')), may hold values from -0.3125 to 0.3125
- w_key: float32 [768, 768], P(('dp', 'fsdp')), may hold values from -0.21875 to 0.21875
- w_value: float32 [768, 768], P(('dp', 'fsdp')), may hold values from -0.21875 to 0.21875
- w_output: float32 [768, 768], P(('dp', 'fsdp')), may hold values from -0.625 to 0.625
- b_query: float32 [768], P(('dp', 'fsdp')), may hold values from -3 to 3
- b_value: float32 [768], P(('dp', 'fsdp')), may hold values from -3 to 3
- b_output: float32 [768], P(('dp', 'fsdp')), may hold values from -3 to 3
- attn_gain: float32 [768], P(('dp', 'fsdp')), may hold values from 0.5 to 1.5
- attn_shift: float32 [768], P(('dp', 'fsdp')), may hold values from -2 to 2
- w_inner: float32 [768, 3072], P(('dp', 'fsdp')), may hold values from -0.21875 to 0.21875
- b_inner: float32 [3072], P(('dp', 'fsdp')), may hold values from -3 to 3
- w_outer: float32 [3072, 768], P(('dp', 'fsdp')), may hold values from -0.109375 to 0.109375
- b_outer: float32 [768], P(('dp', 'fsdp')), may hold values from -2 to 2
- ffn_gain: float32 [768], P(('dp', 'fsdp')), may hold values from 0.5 to 1.5
- ffn_shift: float32 [768], P(('dp', 'fsdp')), may hold values from -2 to 2
Outputs:
- query_loss: float32 [256], P(('dp', 'fsdp'))
- hidden_out: bfloat16 [32, 1024, 768], P(('dp', 'fsdp'))
- hidden_grad: float32 [32, 1024, 768], P(('dp', 'fsdp'))
- w_query_grad: float32 [768, 768], P(('dp', 'fsdp'))
- w_key_grad: float32 [768, 768], P(('dp', 'fsdp'))
- w_value_grad: float32 [768, 768], P(('dp', 'fsdp'))
- w_output_grad: float32 [768, 768], P(('dp', 'fsdp'))
- b_query_grad: float32 [768], P(('dp', 'fsdp'))
- b_value_grad: float32 [768], P(('dp', 'fsdp'))
- b_output_grad: float32 [768], P(('dp', 'fsdp'))
- attn_gain_grad: float32 [768], P(('dp', 'fsdp'))
- attn_shift_grad: float32 [768], P(('dp', 'fsdp'))
- w_inner_grad: float32 [768, 3072], P(('dp', 'fsdp'))
- b_inner_grad: float32 [3072], P(('dp', 'fsdp'))
- w_outer_grad: float32 [3072, 768], P(('dp', 'fsdp'))
- b_outer_grad: float32 [768], P(('dp', 'fsdp'))
- ffn_gain_grad: float32 [768], P(('dp', 'fsdp'))
- ffn_shift_grad: float32 [768], P(('dp', 'fsdp'))
Inputs may be any that keep to these rules, and one draw needn't show every extreme that they name: `segment_ids`: each row holds 16 segments numbered in order of position, a query segment (even number) and a passage segment (odd number) alternating. `query_cls`: the first position of each query segment of the row, in order. `passage_cls`: the first position of each passage segment of the row, in order.
All inputs are finite; a program needn't handle non-finite values.
Results may differ from a plain program's by a relative error of at most 0.013.
The roundings to bfloat16 on the way count: a program that leaves them out, or rounds other values in their place, can miss the bound.
Values may be sent and summed in bfloat16 or wider, within the bound.
No kernel may reach another device: no remote copies, remote signals or barrier semaphores. Data moves between devices by JAX's collectives and lax.ppermute only.
A program may use at most 256 MiB of HBM per device.

v0:
```python
import math
import jax
import jax.numpy as jnp
from jax import lax
from jax.sharding import PartitionSpec as P

HEADS = 12
HEAD = 64
EPS = 1e-12
NEG = -1e30


def matmul(left, right):
    return jnp.dot(left, right, preferred_element_type=jnp.float32)


def contract_rows(left, right):
    return lax.dot_general(
        left, right, (((0,), (0,)), ((), ())), preferred_element_type=jnp.float32
    )


def contract_cols(left, right):
    return lax.dot_general(
        left, right, (((1,), (1,)), ((), ())), preferred_element_type=jnp.float32
    )


def heads_view(block):
    return block.reshape(block.shape[0], HEADS, HEAD)


def norm_forward(value, gain, shift):
    mean = jnp.mean(value, axis=-1, keepdims=True)
    centred = value - mean
    spread = jnp.mean(centred * centred, axis=-1, keepdims=True)
    scaling = lax.rsqrt(spread + EPS)
    normed = centred * scaling
    return (normed * gain + shift, normed, scaling)


def norm_backward(grad, normed, scaling, gain):
    scaled = grad * gain
    first_mean = jnp.mean(scaled, axis=-1, keepdims=True)
    second_mean = jnp.mean(scaled * normed, axis=-1, keepdims=True)
    result = scaling * (scaled - first_mean - normed * second_mean)
    return (result, jnp.sum(grad * normed, axis=0), jnp.sum(grad, axis=0))


def gelu_parts(pre_act):
    cdf_part = 0.5 * (1.0 + lax.erf(pre_act * (1.0 / math.sqrt(2.0))))
    slope = cdf_part + pre_act * jnp.exp(-0.5 * pre_act * pre_act) * (
        1.0 / math.sqrt(2.0 * math.pi)
    )
    return (pre_act * cdf_part, slope)


def block_scores(query_block, key_row, query_segment, key_segment):
    raw_scores = jnp.einsum(
        "qhd,khd->hqk",
        heads_view(query_block),
        heads_view(key_row),
        preferred_element_type=jnp.float32,
    )
    same = query_segment[:, None] == key_segment[None, :]
    return jnp.where(same[None], raw_scores * HEAD ** (-0.5), NEG)


def body(
    hidden_in,
    row_grad,
    segment_ids,
    query_cls,
    passage_cls,
    positives,
    w_query,
    w_key,
    w_value,
    w_output,
    b_query,
    b_value,
    b_output,
    attn_gain,
    attn_shift,
    w_inner,
    b_inner,
    w_outer,
    b_outer,
    ffn_gain,
    ffn_shift,
):
    rows, length, width = hidden_in.shape
    tokens = rows * length
    span = min(512, length)
    per_row = length // span
    inputs = hidden_in.reshape(tokens, width)
    residual_in = inputs.astype(jnp.float32)
    segment_flat = segment_ids.reshape(tokens)
    attn_params = (
        lax.all_gather(w_query.astype(jnp.bfloat16), ("dp", "fsdp"), axis=0, tiled=True),
        lax.all_gather(w_key.astype(jnp.bfloat16), ("dp", "fsdp"), axis=0, tiled=True),
        lax.all_gather(w_value.astype(jnp.bfloat16), ("dp", "fsdp"), axis=0, tiled=True),
        lax.all_gather(w_output.astype(jnp.bfloat16), ("dp", "fsdp"), axis=0, tiled=True),
        lax.all_gather(b_query.astype(jnp.bfloat16), ("dp", "fsdp"), axis=0, tiled=True),
        lax.all_gather(b_value.astype(jnp.bfloat16), ("dp", "fsdp"), axis=0, tiled=True),
        lax.all_gather(b_output.astype(jnp.bfloat16), ("dp", "fsdp"), axis=0, tiled=True),
        lax.all_gather(attn_gain.astype(jnp.bfloat16), ("dp", "fsdp"), axis=0, tiled=True),
        lax.all_gather(attn_shift.astype(jnp.bfloat16), ("dp", "fsdp"), axis=0, tiled=True),
    )
    (
        query_mat,
        key_mat,
        value_mat,
        output_mat,
        query_bias,
        value_bias,
        output_bias,
        gain_one,
        shift_one,
    ) = attn_params
    gain_one = gain_one.astype(jnp.float32)
    queries = (matmul(inputs, query_mat) + query_bias.astype(jnp.float32)).astype(jnp.bfloat16)
    keys_all = matmul(inputs, key_mat).astype(jnp.bfloat16)
    values = (matmul(inputs, value_mat) + value_bias.astype(jnp.float32)).astype(jnp.bfloat16)

    def block_parts(index):
        query_start = index * span
        return (
            lax.dynamic_slice_in_dim(queries, query_start, span, 0),
            keys_all,
            values,
            lax.dynamic_slice_in_dim(segment_flat, query_start, span, 0),
            segment_flat,
            query_start,
        )

    def attend(index):
        query_block, key_row, value_row, query_segment, key_segment, query_start = block_parts(
            index
        )
        scores = block_scores(query_block, key_row, query_segment, key_segment)
        highest = jnp.max(scores, axis=-1, keepdims=True)
        exp_scores = jnp.exp(scores - highest)
        total = jnp.sum(exp_scores, axis=-1, keepdims=True)
        probs = (exp_scores / total).astype(jnp.bfloat16)
        context = jnp.einsum(
            "hqk,khd->qhd", probs, heads_view(value_row), preferred_element_type=jnp.float32
        )
        return (
            context.reshape(span, width).astype(jnp.bfloat16),
            (highest + jnp.log(total))[..., 0],
        )

    block_ids = jnp.arange(rows * per_row, dtype=jnp.int32)
    context_blocks, log_totals = lax.map(attend, block_ids)
    context = context_blocks.reshape(tokens, width)
    branch = matmul(context, output_mat) + output_bias.astype(jnp.float32)
    middle, normed_one, scaling_one = norm_forward(
        residual_in + branch, gain_one, shift_one.astype(jnp.float32)
    )
    middle_low = middle.astype(jnp.bfloat16)
    ffn_params = (
        lax.all_gather(w_inner.astype(jnp.bfloat16), ("dp", "fsdp"), axis=0, tiled=True),
        lax.all_gather(w_outer.astype(jnp.bfloat16), ("dp", "fsdp"), axis=0, tiled=True),
        lax.all_gather(b_inner.astype(jnp.bfloat16), ("dp", "fsdp"), axis=0, tiled=True),
        lax.all_gather(b_outer.astype(jnp.bfloat16), ("dp", "fsdp"), axis=0, tiled=True),
        lax.all_gather(ffn_gain.astype(jnp.bfloat16), ("dp", "fsdp"), axis=0, tiled=True),
        lax.all_gather(ffn_shift.astype(jnp.bfloat16), ("dp", "fsdp"), axis=0, tiled=True),
    )
    inner_mat, outer_mat, inner_bias, outer_bias, gain_two, shift_two = ffn_params
    gain_two = gain_two.astype(jnp.float32)
    pre_act = matmul(middle_low, inner_mat) + inner_bias.astype(jnp.float32)
    activated, slope = gelu_parts(pre_act)
    act_low = activated.astype(jnp.bfloat16)
    update = matmul(act_low, outer_mat) + outer_bias.astype(jnp.float32)
    output, normed_two, scaling_two = norm_forward(
        middle + update, gain_two, shift_two.astype(jnp.float32)
    )
    pairs = query_cls.shape[1]
    count = rows * pairs
    row_base = (jnp.arange(rows, dtype=jnp.int32) * length)[:, None]
    query_index = (query_cls + row_base).reshape(count)
    passage_index = (passage_cls + row_base).reshape(count)
    query_emb = output[query_index].astype(jnp.bfloat16)
    passage_emb = output[passage_index].astype(jnp.bfloat16)
    score_scale = 4.0 / math.sqrt(width)
    all_passages = lax.all_gather(passage_emb, ("dp", "fsdp"), axis=0, tiled=True)
    columns = all_passages.shape[0]
    first = lax.axis_index(("dp", "fsdp")) * count
    scores = contract_cols(query_emb, all_passages) * score_scale
    own_positives = lax.dynamic_slice_in_dim(positives, first, count, 0)
    column_ids = jnp.arange(columns, dtype=jnp.int32)
    hit = (column_ids[None, :] == own_positives[:, None]).astype(jnp.float32)
    highest = jnp.max(scores, axis=-1, keepdims=True)
    log_total = highest[:, 0] + jnp.log(jnp.sum(jnp.exp(scores - highest), axis=-1))
    query_loss = log_total - jnp.sum(hit * scores, axis=-1)
    score_grad = ((jnp.exp(scores - log_total[:, None]) - hit) * score_scale).astype(jnp.bfloat16)
    query_emb_grad = matmul(score_grad, all_passages)
    passage_emb_grad = lax.psum_scatter(
        contract_rows(score_grad, query_emb), ("dp", "fsdp"), scatter_dimension=0, tiled=True
    )
    out_grad = row_grad.reshape(tokens, width).astype(jnp.float32)
    out_grad = out_grad.at[query_index].add(query_emb_grad).at[passage_index].add(passage_emb_grad)
    sum_grad, gain_two_grad, shift_two_grad = norm_backward(
        out_grad, normed_two, scaling_two, gain_two
    )
    update_grad = sum_grad.astype(jnp.bfloat16)
    outer_grad = contract_rows(act_low, update_grad)
    outer_bias_grad = jnp.sum(update_grad.astype(jnp.float32), axis=0)
    pre_grad = (contract_cols(update_grad, outer_mat) * slope).astype(jnp.bfloat16)
    inner_grad = contract_rows(middle_low, pre_grad)
    inner_bias_grad = jnp.sum(pre_grad.astype(jnp.float32), axis=0)
    middle_grad = sum_grad + contract_cols(pre_grad, inner_mat)
    ffn_grads = (
        lax.psum_scatter(inner_grad, ("dp", "fsdp"), scatter_dimension=0, tiled=True),
        lax.psum_scatter(inner_bias_grad, ("dp", "fsdp"), scatter_dimension=0, tiled=True),
        lax.psum_scatter(outer_grad, ("dp", "fsdp"), scatter_dimension=0, tiled=True),
        lax.psum_scatter(outer_bias_grad, ("dp", "fsdp"), scatter_dimension=0, tiled=True),
        lax.psum_scatter(gain_two_grad, ("dp", "fsdp"), scatter_dimension=0, tiled=True),
        lax.psum_scatter(shift_two_grad, ("dp", "fsdp"), scatter_dimension=0, tiled=True),
    )
    first_grad, gain_one_grad, shift_one_grad = norm_backward(
        middle_grad, normed_one, scaling_one, gain_one
    )
    branch_grad = first_grad.astype(jnp.bfloat16)
    output_w_grad = contract_rows(context, branch_grad)
    output_bias_grad = jnp.sum(branch_grad.astype(jnp.float32), axis=0)
    context_grad = contract_cols(branch_grad, output_mat).astype(jnp.bfloat16)

    def attend_back(item):
        index, log_block = item
        query_block, key_row, value_row, query_segment, key_segment, query_start = block_parts(
            index
        )
        context_block = lax.dynamic_slice_in_dim(context_grad, query_start, span, 0)
        scores_again = block_scores(query_block, key_row, query_segment, key_segment)
        probs = jnp.exp(scores_again - log_block[..., None])
        prob_grad = jnp.einsum(
            "qhd,khd->hqk",
            heads_view(context_block),
            heads_view(value_row),
            preferred_element_type=jnp.float32,
        )
        value_part = jnp.einsum(
            "hqk,qhd->khd",
            probs.astype(jnp.bfloat16),
            heads_view(context_block),
            preferred_element_type=jnp.float32,
        )
        inner_sum = jnp.sum(probs * prob_grad, axis=-1, keepdims=True)
        score_part = (probs * (prob_grad - inner_sum)).astype(jnp.bfloat16)
        query_part = jnp.einsum(
            "hqk,khd->qhd", score_part, heads_view(key_row), preferred_element_type=jnp.float32
        ) * HEAD ** (-0.5)
        key_part = jnp.einsum(
            "hqk,qhd->khd", score_part, heads_view(query_block), preferred_element_type=jnp.float32
        ) * HEAD ** (-0.5)
        return (
            query_part.reshape(span, width),
            key_part.reshape(length, width),
            value_part.reshape(length, width),
        )

    query_parts, key_parts, value_parts = lax.map(attend_back, (block_ids, log_totals))
    query_grad = query_parts.reshape(tokens, width).astype(jnp.bfloat16)
    key_grad = (
        key_parts.reshape(rows, per_row, length, width)
        .sum(axis=1)
        .reshape(tokens, width)
        .astype(jnp.bfloat16)
    )
    value_grad = (
        value_parts.reshape(rows, per_row, length, width)
        .sum(axis=1)
        .reshape(tokens, width)
        .astype(jnp.bfloat16)
    )
    query_w_grad = contract_rows(inputs, query_grad)
    key_w_grad = contract_rows(inputs, key_grad)
    value_w_grad = contract_rows(inputs, value_grad)
    query_bias_grad = jnp.sum(query_grad.astype(jnp.float32), axis=0)
    value_bias_grad = jnp.sum(value_grad.astype(jnp.float32), axis=0)
    hidden_grad = (
        first_grad
        + contract_cols(query_grad, query_mat)
        + contract_cols(key_grad, key_mat)
        + contract_cols(value_grad, value_mat)
    )
    attn_grads = (
        lax.psum_scatter(query_w_grad, ("dp", "fsdp"), scatter_dimension=0, tiled=True),
        lax.psum_scatter(key_w_grad, ("dp", "fsdp"), scatter_dimension=0, tiled=True),
        lax.psum_scatter(value_w_grad, ("dp", "fsdp"), scatter_dimension=0, tiled=True),
        lax.psum_scatter(output_w_grad, ("dp", "fsdp"), scatter_dimension=0, tiled=True),
        lax.psum_scatter(query_bias_grad, ("dp", "fsdp"), scatter_dimension=0, tiled=True),
        lax.psum_scatter(value_bias_grad, ("dp", "fsdp"), scatter_dimension=0, tiled=True),
        lax.psum_scatter(output_bias_grad, ("dp", "fsdp"), scatter_dimension=0, tiled=True),
        lax.psum_scatter(gain_one_grad, ("dp", "fsdp"), scatter_dimension=0, tiled=True),
        lax.psum_scatter(shift_one_grad, ("dp", "fsdp"), scatter_dimension=0, tiled=True),
    )
    hidden_out = output.reshape(rows, length, width).astype(jnp.bfloat16)
    return (
        (query_loss, hidden_out, hidden_grad.reshape(rows, length, width))
        + tuple(attn_grads)
        + tuple(ffn_grads)
    )


def solution(mesh):
    placed = (
        P(("dp", "fsdp"), None, None),
        P(("dp", "fsdp"), None, None),
        P(("dp", "fsdp"), None),
        P(("dp", "fsdp"), None),
        P(("dp", "fsdp"), None),
        P(),
        P(("dp", "fsdp"), None),
        P(("dp", "fsdp"), None),
        P(("dp", "fsdp"), None),
        P(("dp", "fsdp"), None),
        P(("dp", "fsdp")),
        P(("dp", "fsdp")),
        P(("dp", "fsdp")),
        P(("dp", "fsdp")),
        P(("dp", "fsdp")),
        P(("dp", "fsdp"), None),
        P(("dp", "fsdp")),
        P(("dp", "fsdp"), None),
        P(("dp", "fsdp")),
        P(("dp", "fsdp")),
        P(("dp", "fsdp")),
    )
    return jax.shard_map(
        body,
        mesh=mesh,
        in_specs=placed,
        out_specs=(
            P(("dp", "fsdp")),
            P(("dp", "fsdp"), None, None),
            P(("dp", "fsdp"), None, None),
            P(("dp", "fsdp"), None),
            P(("dp", "fsdp"), None),
            P(("dp", "fsdp"), None),
            P(("dp", "fsdp"), None),
            P(("dp", "fsdp")),
            P(("dp", "fsdp")),
            P(("dp", "fsdp")),
            P(("dp", "fsdp")),
            P(("dp", "fsdp")),
            P(("dp", "fsdp"), None),
            P(("dp", "fsdp")),
            P(("dp", "fsdp"), None),
            P(("dp", "fsdp")),
            P(("dp", "fsdp")),
            P(("dp", "fsdp")),
        ),
        check_vma=False,
    )
```

profile of v0, /device:TPU:0, one launch (start us, length us, event | category | flops | bytes accessed | tf_op | source)
XLA Modules:
  0.0 1375.4 jit_solution(13707741930182174458)
XLA Ops:
  27.5 43.0 %all-reduce.19 = (bf16[768]{0:T(1024)(128)(2,1)S(1)}, bf16[768]{0:T(1024)(128)(2,1)S(1)}, bf16[768]{0:T(1024)(128)(2,1)S(1)}, bf16[768]{0:T(1024)(128)(2,1)S(1)}...) all-reduce(bf16[768]{0:T(1024)(128)(2,1)S(1)} %dynamic-update-slice, ...), channel_id=1, replica_groups=mesh['dp'=16,'fsdp'=2] {'dp','fsdp'}, use_global_device_ids=true, to_apply=%add | all-reduce | flops 9216 | bytes 36864
  82.2 42.4 %all-gather.7.cloned.1.call-done = bf16[768,768]{1,0:T(8,128)(2,1)} async-done(((bf16[24,768]{1,0:T(8,128)(2,1)}), bf16[768,768]{1,0:T(8,128)(2,1)}) %all-gather.7.cloned.1.call-update) | async-done | bytes 1179664 | tf_op jit(solution)/shard_map/all_gather | solution.py:100
  130.2 50.8 %all-gather.9.cloned.1.call-done = bf16[768,768]{1,0:T(8,128)(2,1)} async-done(((bf16[24,768]{1,0:T(8,128)(2,1)}), bf16[768,768]{1,0:T(8,128)(2,1)}) %all-gather.9.cloned.1.call-update) | async-done | bytes 1179664 | tf_op jit(solution)/shard_map/all_gather | solution.py:101
  187.8 79.4 %while.26 = (s32[]{:T(128)}, bf16[2,512,768]{2,1,0:T(8,128)(2,1)}, f32[2,12,512]{2,1,0:T(8,128)S(1)}, s32[2]{0:T(128)S(1)}, s32[1024]{0:T(1024)S(1)}, /*index=5*...) while((s32[]{:T(128)}, bf16[2,512,768]{2,1,0:T(8,128)(2,1)}, ...), condition=%wide.region_3.4_spmd, body=%wide.region_0.3_spmd.sunk | while | flops 1687021568 | bytes 187926768 | solution.py:155
  201.7 12.3 fusion.116
  241.2 12.3 fusion.116
  273.8 29.2 %all-gather.15.cloned.1.call-done = bf16[768,3072]{1,0:T(8,128)(2,1)} async-done(((bf16[24,3072]{1,0:T(8,128)(2,1)}), bf16[768,3072]{1,0:T(8,128)(2,1)}) %all-gather.15.cloned.1.call-update) | async-done | bytes 4718608 | tf_op jit(solution)/shard_map/all_gather | solution.py:163
  303.1 13.6 multiply_convert_fusion.1
  316.7 51.6 %all-gather.17.cloned.1.call-done = bf16[3072,768]{1,0:T(8,128)(2,1)} async-done(((bf16[96,768]{1,0:T(8,128)(2,1)}), bf16[3072,768]{1,0:T(8,128)(2,1)}) %all-gather.17.cloned.1.call-update) | async-done | bytes 4718608 | tf_op jit(solution)/shard_map/all_gather | solution.py:164
  388.6 40.1 %all_gather.63 = bf16[256,768]{1,0:T(8,128)(2,1)S(1)} all-gather(bf16[8,768]{1,0:T(8,128)(2,1)} %gather_fusion.1), channel_id=1, replica_groups=mesh['dp'=16,'fsdp'=2] {'dp','fsdp'}, dimensions={0}, use_global_device_ids=true | all-gather | bytes 405504 | tf_op jit(solution)/shard_map/all_gather | solution.py:187
  442.3 84.0 %reduce-scatter.14.cloned.1.call-done = f32[8,768]{1,0:T(8,128)} async-done(((f32[256,768]{1,0:T(8,128)}), f32[8,768]{1,0:T(8,128)}) %reduce-scatter.14.cloned.1.call-update) | async-done | bytes 24592 | tf_op jit(solution)/shard_map/reduce_scatter | solution.py:199
  540.0 13.8 %convert_reduce_fusion = (f32[3072]{0:T(1024)}, bf16[1024,3072]{1,0:T(8,128)(2,1)S(1)}) fusion(f32[1024,3072]{1,0:T(8,128)} %get-tuple-element.336, f32[3072]{0:T(1024)S(1)} %copy-done.47, bf16[3072,768]{1,0:T(8,128)(2,1)} %all-gather.17.cloned.1.call-done, f32[1024,768]{0,1:T(8,128)S(1)} %get-tuple-element.322), kind=kOutput, calls=%fused_computation.41 | convolution fusion | flops 4873516032 | bytes 26763264 | tf_op jit(solution)/shard_map/dot_general | solution.py:24
  569.0 198.2 %while.27 = (s32[]{:T(128)}, bf16[2,512,768]{2,1,0:T(8,128)(2,1)}, f32[2,1024,768]{1,2,0:T(8,128)}, f32[2,1024,768]{1,2,0:T(8,128)}, s32[2]{0:T(128)S(1)}, /*ind...) while((s32[]{:T(128)}, bf16[2,512,768]{2,1,0:T(8,128)(2,1)}, ...), condition=%wide.region_20.21_spmd, body=%wide.region_18.20_spmd.sunk | while | flops 4122994688 | bytes 229558544 | solution.py:264
  586.3 13.4 fusion.129
  599.7 20.3 %multiply_reduce_fusion.10 = (f32[12,512]{1,0:T(8,128)S(1)}, f32[12,512,1024]{2,1,0:T(8,128)}) fusion(f32[12,512,1024]{2,1,0:T(8,128)} %fusion.128, f32[12,512]{1,0:T(8,128)S(1)} %dynamic-slice_bitcast_fusion.2, pred[512,1024]{1,0:T(8,128)(4,1)S(1)} %broadcast_compare_fusion.5, bf16[512,12,64]{0,2,1:T(8,128)(2,1)S(1)} %bitcast.180, ...), kind=kOutput, calls=%fused_computation.18.clone.1 | convolution fusion | flops 836757504 | bytes 53264384 | tf_op jit(solution)/shard_map/while/body/eval_jaxpr/qhd,khd->hqk/dot_general | solution.py:238
  620.0 22.1 %multiply_convert_fusion.6 = bf16[12,512,1024]{2,1,0:T(8,128)(2,1)} fusion(f32[12,512,1024]{2,1,0:T(8,128)} %get-tuple-element.482, f32[12,512,1024]{2,1,0:T(8,128)} %fusion.128, f32[12,512]{1,0:T(8,128)S(1)} %get-tuple-element.483, f32[12,512]{1,0:T(8,128)S(1)} %dynamic-slice_bitcast_fusion.2, pred[512,1024]{1,0:T(8,128)(4,1)S(1)} %broadcast_compare_fusion.5), kind=kLoop, calls=%fused_computation.17.clone.1 | loop fusion | flops 37748736 | bytes 63488000 | tf_op jit(solution)/shard_map/while/body/eval_jaxpr/convert_element_type | solution.py:251
  685.7 13.1 fusion.129
  698.8 20.2 %multiply_reduce_fusion.10 = (f32[12,512]{1,0:T(8,128)S(1)}, f32[12,512,1024]{2,1,0:T(8,128)}) fusion(f32[12,512,1024]{2,1,0:T(8,128)} %fusion.128, f32[12,512]{1,0:T(8,128)S(1)} %dynamic-slice_bitcast_fusion.2, pred[512,1024]{1,0:T(8,128)(4,1)S(1)} %broadcast_compare_fusion.5, bf16[512,12,64]{0,2,1:T(8,128)(2,1)S(1)} %bitcast.180, ...), kind=kOutput, calls=%fused_computation.18.clone.1 | convolution fusion | flops 836757504 | bytes 53264384 | tf_op jit(solution)/shard_map/while/body/eval_jaxpr/qhd,khd->hqk/dot_general | solution.py:238
  719.0 21.3 %multiply_convert_fusion.6 = bf16[12,512,1024]{2,1,0:T(8,128)(2,1)} fusion(f32[12,512,1024]{2,1,0:T(8,128)} %get-tuple-element.482, f32[12,512,1024]{2,1,0:T(8,128)} %fusion.128, f32[12,512]{1,0:T(8,128)S(1)} %get-tuple-element.483, f32[12,512]{1,0:T(8,128)S(1)} %dynamic-slice_bitcast_fusion.2, pred[512,1024]{1,0:T(8,128)(4,1)S(1)} %broadcast_compare_fusion.5), kind=kLoop, calls=%fused_computation.17.clone.1 | loop fusion | flops 37748736 | bytes 63488000 | tf_op jit(solution)/shard_map/while/body/eval_jaxpr/convert_element_type | solution.py:251
  828.6 41.0 %all-reduce.18 = (f32[768]{0:T(1024)S(1)}, f32[768]{0:T(1024)S(1)}, f32[768]{0:T(1024)S(1)}, f32[768]{0:T(1024)S(1)}, f32[768]{0:T(1024)S(1)}, /*index=5*/f32[30...) all-reduce(f32[768]{0:T(1024)S(1)} %convert_reduce_fusion.4, ...), channel_id=7, replica_groups=mesh['dp'=16,'fsdp'=2] {'dp','fsdp'}, use_global_device_ids=true, to_apply=%region_28.29.clone | all-reduce | flops 9216 | bytes 73728
  883.2 97.8 %reduce-scatter.26.cloned.1.call-done = f32[24,768]{1,0:T(8,128)} async-done(((f32[768,768]{1,0:T(8,128)}), f32[24,768]{1,0:T(8,128)}) %reduce-scatter.26.cloned.1.call-update) | async-done | bytes 73744
  980.9 104.5 %reduce-scatter.22.cloned.1.call-done = f32[24,768]{1,0:T(8,128)} async-done(((f32[768,768]{1,0:T(8,128)}), f32[24,768]{1,0:T(8,128)}) %reduce-scatter.22.cloned.1.call-update) | async-done | bytes 73744
  1085.5 141.5 %reduce-scatter.20.cloned.1.call-done = f32[96,768]{1,0:T(8,128)} async-done(((f32[3072,768]{1,0:T(8,128)}), f32[96,768]{1,0:T(8,128)}) %reduce-scatter.20.cloned.1.call-update) | async-done | bytes 294928 | tf_op jit(solution)/shard_map/reduce_scatter | solution.py:217
  1227.0 141.6 %reduce-scatter.18.cloned.1.call-done = f32[24,3072]{1,0:T(8,128)} async-done(((f32[768,3072]{1,0:T(8,128)}), f32[24,3072]{1,0:T(8,128)}) %reduce-scatter.18.cloned.1.call-update) | async-done | bytes 294928 | tf_op jit(solution)/shard_map/reduce_scatter | solution.py:215
  (332 shorter events, 327.0 us)
Async XLA Ops:
  7.2 70.7 %copy-start.16 = (bf16[1,1024,768]{2,1,0:T(8,128)(2,1)S(1)}, bf16[1,1024,768]{2,1,0:T(8,128)(2,1)}, u32[]{:S(2)}) copy-start(bf16[1,1024,768]{2,1,0:T(8,128)(2,1)} %param.25) | copy-start | bytes 4718596
  7.2 70.1 %copy-start.63 = (s32[256]{0:T(256)S(1)}, s32[256]{0:T(256)}, u32[]{:S(2)}) copy-start(s32[256]{0:T(256)} %param.30) | copy-start | bytes 3076
  7.2 70.6 %all-gather.11.cloned.1.call-start = ((), (), s32[]{:S(2)}) async-start(), calls=%async_computation.9 | async-start | bytes 1216512 | tf_op jit(solution)/shard_map/all_gather | solution.py:102
  8.9 115.7 %all-gather.7.cloned.1.call-start = ((), (), s32[]{:S(2)}) async-start(), calls=%async_computation.7 | async-start | bytes 1216512 | tf_op jit(solution)/shard_map/all_gather | solution.py:100
  10.5 170.5 %all-gather.9.cloned.1.call-start = ((), (), s32[]{:S(2)}) async-start(), calls=%async_computation.8 | async-start | bytes 1216512 | tf_op jit(solution)/shard_map/all_gather | solution.py:101
  12.1 255.2 %all-gather.13.cloned.1.call-start = ((), (), s32[]{:S(2)}) async-start(), calls=%async_computation.10 | async-start | bytes 1216512 | tf_op jit(solution)/shard_map/all_gather | solution.py:103
  13.6 289.4 %all-gather.15.cloned.1.call-start = ((), (), s32[]{:S(2)}) async-start(), calls=%async_computation.11 | async-start | bytes 4866048 | tf_op jit(solution)/shard_map/all_gather | solution.py:163
  15.4 353.0 %all-gather.17.cloned.1.call-start = ((), (), s32[]{:S(2)}) async-start(), calls=%async_computation.12 | async-start | bytes 4866048 | tf_op jit(solution)/shard_map/all_gather | solution.py:164
  17.1 509.2 %reduce-scatter.14.cloned.1.call-start = ((), (), s32[]{:S(2)}) async-start(), calls=%async_computation.13 | async-start | bytes 811008 | tf_op jit(solution)/shard_map/reduce_scatter | solution.py:199
  187.8 79.4 %copy-start.52 = (f32[768]{0:T(1024)S(1)}, f32[768]{0:T(1024)}, u32[]{:S(2)}) copy-start(f32[768]{0:T(1024)} %convert_element_type.202) | copy-start | bytes 9220
  271.8 96.5 %copy-start.34 = (f32[1024]{0:T(1024)}, f32[1024]{0:T(1024)S(1)}, u32[]{:S(2)}) copy-start(f32[1024]{0:T(1024)S(1)} %broadcast_multiply_fusion.5) | copy-start | bytes 12292
  273.8 94.5 %copy-start.40 = (f32[1024]{0:T(1024)}, f32[1024]{0:T(1024)S(1)}, u32[]{:S(2)}) copy-start(f32[1024]{0:T(1024)S(1)} %add_rsqrt_fusion.1) | copy-start | bytes 12292
  273.8 94.5 %copy-start.51 = (f32[768]{0:T(1024)S(1)}, f32[768]{0:T(1024)}, u32[]{:S(2)}) copy-start(f32[768]{0:T(1024)} %convert_element_type.214) | copy-start | bytes 9220
  377.8 160.3 %copy-start.2 = (f32[1024,768]{0,1:T(8,128)}, f32[1024,768]{0,1:T(8,128)S(1)}, u32[]{:S(2)}) copy-start(f32[1024,768]{0,1:T(8,128)S(1)} %get-tuple-element.338) | copy-start | bytes 9437188
  377.8 160.3 %copy-start.24 = (f32[1024]{0:T(1024)}, f32[1024]{0:T(1024)S(1)}, u32[]{:S(2)}) copy-start(f32[1024]{0:T(1024)S(1)} %broadcast_multiply_fusion.4) | copy-start | bytes 12292
  378.5 159.6 %copy-start.28 = (f32[1024]{0:T(1024)}, f32[1024]{0:T(1024)S(1)}, u32[]{:S(2)}) copy-start(f32[1024]{0:T(1024)S(1)} %add_rsqrt_fusion) | copy-start | bytes 12292
  433.7 449.4 %reduce-scatter.16.cloned.1.call-start = ((), (), s32[]{:S(2)}) async-start(), calls=%async_computation.14 | async-start | bytes 2433024 | tf_op jit(solution)/shard_map/reduce_scatter | solution.py:293
  565.1 318.0 %reduce-scatter.24.cloned.1.call-start = ((), (), s32[]{:S(2)}) async-start(), calls=%async_computation.18 | async-start | bytes 2433024
  777.6 203.4 %reduce-scatter.26.cloned.1.call-start = ((), (), s32[]{:S(2)}) async-start(), calls=%async_computation.19 | async-start | bytes 2433024
  787.5 297.9 %reduce-scatter.22.cloned.1.call-start = ((), (), s32[]{:S(2)}) async-start(), calls=%async_computation.17 | async-start | bytes 2433024
  795.2 431.7 %reduce-scatter.20.cloned.1.call-start = ((), (), s32[]{:S(2)}) async-start(), calls=%async_computation.16 | async-start | bytes 9732096 | tf_op jit(solution)/shard_map/reduce_scatter | solution.py:217
  805.7 562.8 %reduce-scatter.18.cloned.1.call-start = ((), (), s32[]{:S(2)}) async-start(), calls=%async_computation.15 | async-start | bytes 9732096 | tf_op jit(solution)/shard_map/reduce_scatter | solution.py:215
  825.0 49.3 %copy-start.19 = (bf16[1024,768]{0,1:T(8,128)(2,1)S(1)}, bf16[1024,768]{0,1:T(8,128)(2,1)}, u32[]{:S(2)}) copy-start(bf16[1024,768]{0,1:T(8,128)(2,1)} %reduce_sum.217) | copy-start | bytes 4718596
  825.0 49.3 %copy-start.62 = (bf16[768,768]{1,0:T(8,128)(2,1)S(1)}, bf16[768,768]{1,0:T(8,128)(2,1)}, u32[]{:S(2)}) copy-start(bf16[768,768]{1,0:T(8,128)(2,1)} %all-gather.9.cloned.1.call-done) | copy-start | bytes 3538948
  (58 other events, 355.3 us)
Sparse Core Ops, SparseCore 0:
  11.5 56.7 all-gather.10
  71.7 52.8 all-gather.6
  128.1 52.8 all-gather.8
  184.3 52.8 all-gather.12
  240.5 62.5 all-gather.14
  306.4 61.9 all-gather.16
  433.9 92.3 reduce-scatter.13
  565.2 98.6 reduce-scatter.15
  777.7 98.8 reduce-scatter.23
  882.3 98.6 reduce-scatter.25
  986.8 98.6 reduce-scatter.21
  1091.8 135.1 reduce-scatter.19
  1233.4 135.0 reduce-scatter.17
where the time goes:
time: 1380 us
  waiting for transfers between devices  744 us (54%)
  matrix products  272 us (20%)
  other arithmetic  129 us (9%)
  blocking collectives  124 us (9%)
  local copies, waits for them, and re-layouts  88.3 us (6%)
  between operations  14.9 us (1%)
    unnamed x16, waiting for transfers between devices  203 us
    reduce_scatter x1, waiting for transfers between devices, body(): lax.psum_scatter(inner_grad, ('dp', 'fsdp'), scatter_dimension=0, tiled=T...  142 us
    reduce_scatter x1, waiting for transfers between devices, body(): lax.psum_scatter(outer_grad, ('dp', 'fsdp'), scatter_dimension=0, tiled=T...  142 us
    unnamed x2, blocking collectives  84 us
    reduce_scatter x1, waiting for transfers between devices, body(): lax.psum_scatter(contract_rows(score_grad, query_emb), ('dp', 'fsdp'), sc...  84 us
    all_gather x1, waiting for transfers between devices, body(): lax.all_gather(w_outer.astype(jnp.bfloat16), ('dp', 'fsdp'), axis=0, tile...  51.6 us
    all_gather x1, waiting for transfers between devices, body(): lax.all_gather(w_key.astype(jnp.bfloat16), ('dp', 'fsdp'), axis=0, tiled=...  50.8 us
    dot_general x4, matrix products, block_scores(): jnp.einsum('qhd,khd->hqk', heads_view(query_block), heads_view(key_row),...  47.6 us
  transfers between devices with their start and end apart: 13, of which 9 were waited for; matrix products, arithmetic and copies ran while one was open for 30% of the time, Pallas kernels for 0%

commit v1 on v0

--- a/solution.py
+++ b/solution.py
@@ -1,3 +1,4 @@
+import functools
 import math
 import jax
 import jax.numpy as jnp
@@ -8,6 +9,28 @@
 HEAD = 64
 EPS = 1e-12
 NEG = -1e30
+
+
+def return_all_modes(a0, named_axis):
+    heard, shaped, e_now = (lax.axis_size(named_axis), lax.axis_index(named_axis), a0.shape[0])
+    outcome_arr, local_now = (a0, 1)
+    while local_now < heard:
+        outcome_arr = jnp.concatenate(
+            [
+                outcome_arr,
+                lax.ppermute(
+                    outcome_arr,
+                    named_axis,
+                    tuple(((jj, (jj - local_now) % heard) for jj in range(heard))),
+                ),
+            ],
+            axis=0,
+        )
+        local_now = 2 * local_now
+    return jnp.roll(outcome_arr, shaped * e_now, axis=0)
+
+
+panel_store = functools.partial(return_all_modes, named_axis=("dp", "fsdp"))
 
 
 def matmul(left, right):
@@ -97,7 +120,7 @@
     residual_in = inputs.astype(jnp.float32)
     segment_flat = segment_ids.reshape(tokens)
     attn_params = (
-        lax.all_gather(w_query.astype(jnp.bfloat16), ("dp", "fsdp"), axis=0, tiled=True),
+        panel_store(w_query.astype(jnp.bfloat16)),
         lax.all_gather(w_key.astype(jnp.bfloat16), ("dp", "fsdp"), axis=0, tiled=True),
         lax.all_gather(w_value.astype(jnp.bfloat16), ("dp", "fsdp"), axis=0, tiled=True),
         lax.all_gather(w_output.astype(jnp.bfloat16), ("dp", "fsdp"), axis=0, tiled=True),

time: 1380 us -> 1340 us (0.971)
  waiting for transfers between devices: 744 us -> 688 us
    all_gather x1, waiting for transfers between devices: 50.8 us -> 0.01 us  [body(): lax.all_gather(w_key.astype(jnp.bfloat16), ('dp', 'fsdp'), axis=0, tiled=...]
    all_gather x1 -> x0, waiting for transfers between devices: 42.4 us -> none  [body(): lax.all_gather(w_query.astype(jnp.bfloat16), ('dp', 'fsdp'), axis=0, tile...]
    ppermute x0 -> x5, waiting for transfers between devices: none -> 39.6 us  [return_all_modes(): lax.ppermute(outcome_arr, named_axis, tuple(((jj, (jj - local_now) % hear...]
    unnamed x163 -> x181, local copies, waits for them, and re-layouts: 31.1 us -> 34.3 us
    unnamed x16 -> x15, waiting for transfers between devices: 203 us -> 203 us
  transfers between devices with their start and end apart: 13 -> 17, of which waited for: 9 -> 11; matrix products, arithmetic and copies ran while one was open for 30% -> 30% of each run, Pallas kernels for 0% -> 0%
where the time goes in v1:
time: 1340 us; the launch traced here: 1330 us
  waiting for transfers between devices  688 us (51%)
  matrix products  271 us (20%)
  other arithmetic  126 us (9%)
  blocking collectives  126 us (9%)
  local copies, waits for them, and re-layouts  91.3 us (7%)
  between operations  15.5 us (1%)
    unnamed x15, waiting for transfers between devices  203 us
    reduce_scatter x1, waiting for transfers between devices, body(): lax.psum_scatter(outer_grad, ('dp', 'fsdp'), scatter_dimension=0, tiled=T...  142 us
    reduce_scatter x1, waiting for transfers between devices, body(): lax.psum_scatter(inner_grad, ('dp', 'fsdp'), scatter_dimension=0, tiled=T...  141 us
    unnamed x2, blocking collectives  85.4 us
    reduce_scatter x1, waiting for transfers between devices, body(): lax.psum_scatter(contract_rows(score_grad, query_emb), ('dp', 'fsdp'), sc...  84 us
    all_gather x1, waiting for transfers between devices, body(): lax.all_gather(w_outer.astype(jnp.bfloat16), ('dp', 'fsdp'), axis=0, tile...  51.5 us
    dot_general x4, matrix products, block_scores(): jnp.einsum('qhd,khd->hqk', heads_view(query_block), heads_view(key_row),...  47.6 us
    convert_element_type x2, other arithmetic, attend_back(): score_part = (probs * (prob_grad - inner_sum)).astype(jnp.bfloat16)  43.3 us
  transfers between devices with their start and end apart: 17, of which 11 were waited for; matrix products, arithmetic and copies ran while one was open for 30% of the time, Pallas kernels for 0%

profile of v1, /device:TPU:0, one launch (start us, length us, event | category | flops | bytes accessed | tf_op | source)
XLA Modules:
  0.0 1331.8 jit_solution(15138514052185014135)
XLA Ops:
  37.3 44.3 %all-reduce.19 = (bf16[768]{0:T(1024)(128)(2,1)S(1)}, bf16[768]{0:T(1024)(128)(2,1)S(1)}, bf16[768]{0:T(1024)(128)(2,1)S(1)}, bf16[768]{0:T(1024)(128)(2,1)S(1)}...) all-reduce(bf16[768]{0:T(1024)(128)(2,1)S(1)} %dynamic-update-slice, ...), channel_id=1, replica_groups=mesh['dp'=16,'fsdp'=2] {'dp','fsdp'}, use_global_device_ids=true, to_apply=%add | all-reduce | flops 9216 | bytes 36864
  100.5 26.9 %collective-permute-done.4 = bf16[384,768]{1,0:T(8,128)(2,1)S(1)} collective-permute-done((bf16[384,768]{1,0:T(8,128)(2,1)S(1)}, bf16[384,768]{1,0:T(8,128)(2,1)S(1)}, u32[]{:S(2)}, u32[]{:S(2)}) %collective-permute-start.4) | collective-permute-done | bytes 589856 | tf_op jit(solution)/shard_map/ppermute | solution.py:21
  146.3 79.2 %while.26 = (s32[]{:T(128)}, bf16[2,512,768]{2,1,0:T(8,128)(2,1)}, f32[2,12,512]{2,1,0:T(8,128)S(1)}, s32[2]{0:T(128)S(1)}, s32[1024]{0:T(1024)S(1)}, /*index=5*...) while((s32[]{:T(128)}, bf16[2,512,768]{2,1,0:T(8,128)(2,1)}, ...), condition=%wide.region_3.4_spmd, body=%wide.region_0.3_spmd.sunk | while | flops 1687021568 | bytes 187926768 | solution.py:178
  160.2 12.3 fusion.122
  187.6 12.1 fusion.121
  199.7 12.4 fusion.122
  232.1 26.6 %all-gather.12.cloned.1.call-done = bf16[768,3072]{1,0:T(8,128)(2,1)} async-done(((bf16[24,3072]{1,0:T(8,128)(2,1)}), bf16[768,3072]{1,0:T(8,128)(2,1)}) %all-gather.12.cloned.1.call-update) | async-done | bytes 4718608 | tf_op jit(solution)/shard_map/all_gather | solution.py:186
  258.7 13.8 %multiply_convert_fusion.1 = (bf16[1024,3072]{1,0:T(8,128)(2,1)}, f32[1024,3072]{1,0:T(8,128)}) fusion(f32[3072]{0:T(1024)S(1)} %copy-done.48, bf16[768,3072]{1,0:T(8,128)(2,1)} %all-gather.12.cloned.1.call-done, f32[1024,768]{0,1:T(8,128)} %copy-done.9, f32[768]{0:T(1024)S(1)} %copy-done.51, f32[768]{0:T(1024)S(1)} %copy-done.39, ...), kind=kOutput, calls=%fused_computation.42 | convolution fusion | flops 4854644736 | bytes 26765312 | tf_op jit(solution)/shard_map/dot_general | solution.py:37
  272.5 51.5 %all-gather.14.cloned.1.call-done = bf16[3072,768]{1,0:T(8,128)(2,1)} async-done(((bf16[96,768]{1,0:T(8,128)(2,1)}), bf16[3072,768]{1,0:T(8,128)(2,1)}) %all-gather.14.cloned.1.call-update) | async-done | bytes 4718608 | tf_op jit(solution)/shard_map/all_gather | solution.py:187
  344.2 40.1 %all_gather.59 = bf16[256,768]{1,0:T(8,128)(2,1)S(1)} all-gather(bf16[8,768]{1,0:T(8,128)(2,1)} %gather_fusion.1), channel_id=1, replica_groups=mesh['dp'=16,'fsdp'=2] {'dp','fsdp'}, dimensions={0}, use_global_device_ids=true | all-gather | bytes 405504 | tf_op jit(solution)/shard_map/all_gather | solution.py:210
  397.9 84.0 %reduce-scatter.14.cloned.1.call-done = f32[8,768]{1,0:T(8,128)} async-done(((f32[256,768]{1,0:T(8,128)}), f32[8,768]{1,0:T(8,128)}) %reduce-scatter.14.cloned.1.call-update) | async-done | bytes 24592 | tf_op jit(solution)/shard_map/reduce_scatter | solution.py:222
  495.6 13.8 %convert_reduce_fusion = (f32[3072]{0:T(1024)}, bf16[1024,3072]{1,0:T(8,128)(2,1)S(1)}) fusion(f32[1024,3072]{1,0:T(8,128)} %get-tuple-element.346, f32[3072]{0:T(1024)S(1)} %copy-done.49, bf16[3072,768]{1,0:T(8,128)(2,1)} %all-gather.14.cloned.1.call-done, f32[1024,768]{0,1:T(8,128)S(1)} %get-tuple-element.322), kind=kOutput, calls=%fused_computation.41 | convolution fusion | flops 4873516032 | bytes 26763264 | tf_op jit(solution)/shard_map/dot_general | solution.py:47
  524.7 198.2 %while.27 = (s32[]{:T(128)}, bf16[2,512,768]{2,1,0:T(8,128)(2,1)}, f32[2,1024,768]{1,2,0:T(8,128)}, f32[2,1024,768]{1,2,0:T(8,128)}, s32[2]{0:T(128)S(1)}, /*ind...) while((s32[]{:T(128)}, bf16[2,512,768]{2,1,0:T(8,128)(2,1)}, ...), condition=%wide.region_20.21_spmd, body=%wide.region_18.20_spmd.sunk | while | flops 4122994688 | bytes 229558544 | solution.py:287
  542.0 13.4 %fusion.135 = f32[12,64,1024]{2,1,0:T(8,128)} fusion(bf16[512,12,64]{0,2,1:T(8,128)(2,1)S(1)} %bitcast.181, f32[12,512,1024]{2,1,0:T(8,128)} %fusion.134, f32[12,512]{1,0:T(8,128)S(1)} %dynamic-slice_bitcast_fusion.2, pred[512,1024]{1,0:T(8,128)(4,1)S(1)} %broadcast_compare_fusion.5), kind=kOutput, calls=%fused_computation.21.clone.1 | convolution fusion | flops 830472192 | bytes 29646848 | tf_op jit(solution)/shard_map/while/body/eval_jaxpr/hqk,qhd->khd/dot_general | solution.py:267
  555.4 20.3 %multiply_reduce_fusion.10 = (f32[12,512]{1,0:T(8,128)S(1)}, f32[12,512,1024]{2,1,0:T(8,128)}) fusion(f32[12,512,1024]{2,1,0:T(8,128)} %fusion.134, f32[12,512]{1,0:T(8,128)S(1)} %dynamic-slice_bitcast_fusion.2, pred[512,1024]{1,0:T(8,128)(4,1)S(1)} %broadcast_compare_fusion.5, bf16[512,12,64]{0,2,1:T(8,128)(2,1)S(1)} %bitcast.182, ...), kind=kOutput, calls=%fused_computation.18.clone.1 | convolution fusion | flops 836757504 | bytes 53264384 | tf_op jit(solution)/shard_map/while/body/eval_jaxpr/qhd,khd->hqk/dot_general | solution.py:261
  575.6 22.1 %multiply_convert_fusion.6 = bf16[12,512,1024]{2,1,0:T(8,128)(2,1)} fusion(f32[12,512,1024]{2,1,0:T(8,128)} %get-tuple-element.492, f32[12,512,1024]{2,1,0:T(8,128)} %fusion.134, f32[12,512]{1,0:T(8,128)S(1)} %get-tuple-element.493, f32[12,512]{1,0:T(8,128)S(1)} %dynamic-slice_bitcast_fusion.2, pred[512,1024]{1,0:T(8,128)(4,1)S(1)} %broadcast_compare_fusion.5), kind=kLoop, calls=%fused_computation.17.clone.1 | loop fusion | flops 37748736 | bytes 63488000 | tf_op jit(solution)/shard_map/while/body/eval_jaxpr/convert_element_type | solution.py:274
  641.4 13.1 fusion.135
  654.5 20.2 %multiply_reduce_fusion.10 = (f32[12,512]{1,0:T(8,128)S(1)}, f32[12,512,1024]{2,1,0:T(8,128)}) fusion(f32[12,512,1024]{2,1,0:T(8,128)} %fusion.134, f32[12,512]{1,0:T(8,128)S(1)} %dynamic-slice_bitcast_fusion.2, pred[512,1024]{1,0:T(8,128)(4,1)S(1)} %broadcast_compare_fusion.5, bf16[512,12,64]{0,2,1:T(8,128)(2,1)S(1)} %bitcast.182, ...), kind=kOutput, calls=%fused_computation.18.clone.1 | convolution fusion | flops 836757504 | bytes 53264384 | tf_op jit(solution)/shard_map/while/body/eval_jaxpr/qhd,khd->hqk/dot_general | solution.py:261
  674.6 21.2 %multiply_convert_fusion.6 = bf16[12,512,1024]{2,1,0:T(8,128)(2,1)} fusion(f32[12,512,1024]{2,1,0:T(8,128)} %get-tuple-element.492, f32[12,512,1024]{2,1,0:T(8,128)} %fusion.134, f32[12,512]{1,0:T(8,128)S(1)} %get-tuple-element.493, f32[12,512]{1,0:T(8,128)S(1)} %dynamic-slice_bitcast_fusion.2, pred[512,1024]{1,0:T(8,128)(4,1)S(1)} %broadcast_compare_fusion.5), kind=kLoop, calls=%fused_computation.17.clone.1 | loop fusion | flops 37748736 | bytes 63488000 | tf_op jit(solution)/shard_map/while/body/eval_jaxpr/convert_element_type | solution.py:274
  783.5 41.1 %all-reduce.18 = (f32[768]{0:T(1024)S(1)}, f32[768]{0:T(1024)S(1)}, f32[768]{0:T(1024)S(1)}, f32[768]{0:T(1024)S(1)}, f32[768]{0:T(1024)S(1)}, /*index=5*/f32[30...) all-reduce(f32[768]{0:T(1024)S(1)} %convert_reduce_fusion.4, ...), channel_id=7, replica_groups=mesh['dp'=16,'fsdp'=2] {'dp','fsdp'}, use_global_device_ids=true, to_apply=%region_28.29.clone | all-reduce | flops 9216 | bytes 73728
  838.5 98.7 %reduce-scatter.22.cloned.1.call-done = f32[24,768]{1,0:T(8,128)} async-done(((f32[768,768]{1,0:T(8,128)}), f32[24,768]{1,0:T(8,128)}) %reduce-scatter.22.cloned.1.call-update) | async-done | bytes 73744
  937.2 104.2 %reduce-scatter.26.cloned.1.call-done = f32[24,768]{1,0:T(8,128)} async-done(((f32[768,768]{1,0:T(8,128)}), f32[24,768]{1,0:T(8,128)}) %reduce-scatter.26.cloned.1.call-update) | async-done | bytes 73744
  1041.4 141.7 %reduce-scatter.20.cloned.1.call-done = f32[96,768]{1,0:T(8,128)} async-done(((f32[3072,768]{1,0:T(8,128)}), f32[96,768]{1,0:T(8,128)}) %reduce-scatter.20.cloned.1.call-update) | async-done | bytes 294928 | tf_op jit(solution)/shard_map/reduce_scatter | solution.py:240
  1183.1 141.4 %reduce-scatter.18.cloned.1.call-done = f32[24,3072]{1,0:T(8,128)} async-done(((f32[768,3072]{1,0:T(8,128)}), f32[24,3072]{1,0:T(8,128)}) %reduce-scatter.18.cloned.1.call-update) | async-done | bytes 294928 | tf_op jit(solution)/shard_map/reduce_scatter | solution.py:238
  (361 shorter events, 338.0 us)
Async XLA Ops:
  7.2 80.2 %copy-start.65 = (s32[256]{0:T(256)S(1)}, s32[256]{0:T(256)}, u32[]{:S(2)}) copy-start(s32[256]{0:T(256)} %param.30) | copy-start | bytes 3076
  7.2 124.7 %all-gather.8.cloned.1.call-start = ((), (), s32[]{:S(2)}) async-start(), calls=%async_computation.8 | async-start | bytes 1216512 | tf_op jit(solution)/shard_map/all_gather | solution.py:125
  8.9 130.5 %all-gather.6.cloned.1.call-start = ((), (), s32[]{:S(2)}) async-start(), calls=%async_computation.7 | async-start | bytes 1216512 | tf_op jit(solution)/shard_map/all_gather | solution.py:124
  10.5 215.1 %all-gather.10.cloned.1.call-start = ((), (), s32[]{:S(2)}) async-start(), calls=%async_computation.9 | async-start | bytes 1216512 | tf_op jit(solution)/shard_map/all_gather | solution.py:126
  12.1 246.6 %all-gather.12.cloned.1.call-start = ((), (), s32[]{:S(2)}) async-start(), calls=%async_computation.10 | async-start | bytes 4866048 | tf_op jit(solution)/shard_map/all_gather | solution.py:186
  13.8 310.2 %all-gather.14.cloned.1.call-start = ((), (), s32[]{:S(2)}) async-start(), calls=%async_computation.11 | async-start | bytes 4866048 | tf_op jit(solution)/shard_map/all_gather | solution.py:187
  14.7 8.0 collective-permute-start
  22.8 4.4 collective-permute-start.1
  27.2 60.8 %collective-permute-start.2 = (bf16[96,768]{1,0:T(8,128)(2,1)S(1)}, bf16[96,768]{1,0:T(8,128)(2,1)S(1)}, u32[]{:S(2)}, u32[]{:S(2)}) collective-permute-start(bf16[96,768]{1,0:T(8,128)(2,1)S(1)} %pad_maximum_fusion.1), channel_id=1, source_target_pairs={{0,28},{1,29},{2,30},{3,31},{4,0},{5,1},{6,2},{7,3},{8,4},{9,5},{1... | collective-permute-start | bytes 442376 | tf_op jit(solution)/shard_map/ppermute | solution.py:21
  29.4 452.5 %reduce-scatter.14.cloned.1.call-start = ((), (), s32[]{:S(2)}) async-start(), calls=%async_computation.12 | async-start | bytes 811008 | tf_op jit(solution)/shard_map/reduce_scatter | solution.py:222
  88.0 9.4 collective-permute-start.3
  97.4 30.0 %collective-permute-start.4 = (bf16[384,768]{1,0:T(8,128)(2,1)S(1)}, bf16[384,768]{1,0:T(8,128)(2,1)S(1)}, u32[]{:S(2)}, u32[]{:S(2)}) collective-permute-start(bf16[384,768]{1,0:T(8,128)(2,1)S(1)} %get-tuple-element.335), channel_id=1, source_target_pairs={{0,16},{1,17},{2,18},{3,19},{4,20},{5,21},{6,22},{7,23},{8,24},{9,... | collective-permute-start | bytes 1769480 | tf_op jit(solution)/shard_map/ppermute | solution.py:21
  230.1 93.9 %copy-start.36 = (f32[1024]{0:T(1024)}, f32[1024]{0:T(1024)S(1)}, u32[]{:S(2)}) copy-start(f32[1024]{0:T(1024)S(1)} %broadcast_multiply_fusion.5) | copy-start | bytes 12292
  232.1 91.9 %copy-start.42 = (f32[1024]{0:T(1024)}, f32[1024]{0:T(1024)S(1)}, u32[]{:S(2)}) copy-start(f32[1024]{0:T(1024)S(1)} %add_rsqrt_fusion.1) | copy-start | bytes 12292
  232.1 91.9 %copy-start.53 = (f32[768]{0:T(1024)S(1)}, f32[768]{0:T(1024)}, u32[]{:S(2)}) copy-start(f32[768]{0:T(1024)} %convert_element_type.218) | copy-start | bytes 9220
  333.4 160.3 %copy-start.2 = (f32[1024,768]{0,1:T(8,128)}, f32[1024,768]{0,1:T(8,128)S(1)}, u32[]{:S(2)}) copy-start(f32[1024,768]{0,1:T(8,128)S(1)} %get-tuple-element.348) | copy-start | bytes 9437188
  333.5 160.3 %copy-start.26 = (f32[1024]{0:T(1024)}, f32[1024]{0:T(1024)S(1)}, u32[]{:S(2)}) copy-start(f32[1024]{0:T(1024)S(1)} %broadcast_multiply_fusion.4) | copy-start | bytes 12292
  334.2 159.6 %copy-start.30 = (f32[1024]{0:T(1024)}, f32[1024]{0:T(1024)S(1)}, u32[]{:S(2)}) copy-start(f32[1024]{0:T(1024)S(1)} %add_rsqrt_fusion) | copy-start | bytes 12292
  389.3 449.2 %reduce-scatter.16.cloned.1.call-start = ((), (), s32[]{:S(2)}) async-start(), calls=%async_computation.13 | async-start | bytes 2433024 | tf_op jit(solution)/shard_map/reduce_scatter | solution.py:316
  520.7 317.8 %reduce-scatter.24.cloned.1.call-start = ((), (), s32[]{:S(2)}) async-start(), calls=%async_computation.17 | async-start | bytes 2433024
  733.9 203.3 %reduce-scatter.22.cloned.1.call-start = ((), (), s32[]{:S(2)}) async-start(), calls=%async_computation.16 | async-start | bytes 2433024
  740.0 301.4 %reduce-scatter.26.cloned.1.call-start = ((), (), s32[]{:S(2)}) async-start(), calls=%async_computation.18 | async-start | bytes 2433024
  750.0 433.1 %reduce-scatter.20.cloned.1.call-start = ((), (), s32[]{:S(2)}) async-start(), calls=%async_computation.15 | async-start | bytes 9732096 | tf_op jit(solution)/shard_map/reduce_scatter | solution.py:240
  760.5 564.0 %reduce-scatter.18.cloned.1.call-start = ((), (), s32[]{:S(2)}) async-start(), calls=%async_computation.14 | async-start | bytes 9732096 | tf_op jit(solution)/shard_map/reduce_scatter | solution.py:238
  (66 other events, 800.2 us)
Sparse Core Ops, SparseCore 0:
  11.5 56.8 all-gather.7
  71.8 64.2 all-gather.5
  139.6 53.1 all-gather.9
  196.1 62.5 all-gather.11
  262.0 61.9 all-gather.13
  389.5 92.3 reduce-scatter.13
  520.9 98.6 reduce-scatter.15
  734.0 98.6 reduce-scatter.23
  838.6 98.5 reduce-scatter.21
  942.9 98.4 reduce-scatter.25
  1047.9 135.1 reduce-scatter.19
  1189.4 135.0 reduce-scatter.17
